TPU v7x, 32 devices: a whole 2x2x4 slice. The times are simulated.
32 devices in a mesh: tower: 4 (over y, x), shard: 8 (over z, core).
Axes of the slice: x: 2, y: 2, z: 4, core: 2. Of those that a mesh axis runs over, the one named last changes fastest.
Arguments:
- pooled: bfloat16 [4, 3072, 48, 128], P('tower', None, 'shard'), may hold values from -6 to 6
- cross_down: bfloat16 [4, 2, 4096, 512], P('tower', None, 'shard'), may hold values from -0.09375 to 0.09375
- cross_up: bfloat16 [4, 2, 512, 4096], P('tower', None, None, 'shard'), may hold values from -0.25 to 0.25
- cross_bias: bfloat16 [4, 2, 4096], P('tower'), may hold values from -3 to 3
- comp_weight: bfloat16 [4, 4096, 256], P('tower', 'shard'), may hold values from -0.09375 to 0.09375
- comp_bias: bfloat16 [4, 256], P('tower'), may hold values from -3 to 3
- over_weight: bfloat16 [1024, 1024], P('tower', 'shard'), may hold values from -0.1875 to 0.1875
- over_bias: bfloat16 [1024], replicated, may hold values from -3 to 3
- table_tower: int32 [128], replicated, may hold values from 0 to 3, as said below
- table_owner: int32 [128], replicated, may hold values from 0 to 7, as said below
Outputs:
- scores: bfloat16 [8, 384, 1024], P('shard', 'tower')
Inputs may be any that keep to these rules, and one draw needn't show every extreme that they name: `table_tower`: each value names exactly 32 tables. `table_owner`: among the tables of one tower no value is named by more than 6 tables, and in every tower some value is named by exactly 6.
All inputs are finite; a program needn't handle non-finite values.
Results may differ from a plain program's by a relative error of at most 0.014.
Values may be sent and summed in bfloat16 or wider, within the bound.
A program may use at most 128 MiB of HBM per device.

v0:
```python
import jax
import jax.numpy as jnp
from jax import lax
from jax.experimental import pallas as pl
from jax.experimental.pallas import tpu as pltpu
from jax.sharding import PartitionSpec as P

MESH = pl.DeviceIdType.MESH
CORES = 2
SIDE = 2
CHUNKS = 6
BF16, F32 = jnp.bfloat16, jnp.float32


def slot_order(table_tower, table_owner, tower_id, per_tower, slot_most):
    table_count = table_tower.shape[0]
    index = jnp.arange(table_count, dtype=jnp.int32)
    inside = table_tower == tower_id
    earlier = index[None, :] < index[:, None]
    before = inside[None, :] & earlier
    position_in = jnp.sum(before.astype(jnp.int32), axis=1)
    same_owner = table_owner[None, :] == table_owner[:, None]
    own_slot = jnp.sum((before & same_owner).astype(jnp.int32), axis=1)
    wanted = table_owner * slot_most + own_slot
    picked = inside[None, :] & (
        position_in[None, :] == jnp.arange(per_tower, dtype=jnp.int32)[:, None]
    )
    return jnp.sum(jnp.where(picked, wanted[None, :], 0), axis=1)


def on_device(
    pooled,
    cross_down,
    cross_up,
    cross_bias,
    comp_weight,
    comp_bias,
    over_weight,
    over_bias,
    table_tower,
    table_owner,
):
    tower_id = lax.axis_index("tower")
    slot_most = pooled.shape[2]
    emb_width = pooled.shape[3]
    feature_count = cross_up.shape[3] * lax.axis_size("shard")
    per_tower = feature_count // emb_width
    received = lax.all_to_all(pooled, "shard", split_axis=1, concat_axis=2, tiled=True)
    wanted = slot_order(table_tower, table_owner, tower_id, per_tower, slot_most)
    tables = jnp.take(received[0], wanted, axis=1)
    sample_count = tables.shape[0]
    base = tables.reshape(sample_count, feature_count)
    state = base
    for section_index in range(cross_down.shape[1]):
        current = state
        lowered = jnp.dot(
            current,
            lax.all_gather(cross_down[0, section_index], "shard", axis=0, tiled=True),
            preferred_element_type=jnp.float32,
        ).astype(jnp.bfloat16)
        raised = jnp.dot(
            lowered,
            lax.all_gather(cross_up[0, section_index], "shard", axis=1, tiled=True),
            preferred_element_type=jnp.float32,
        )
        state = (
            base.astype(jnp.float32) * (raised + cross_bias[0, section_index].astype(jnp.float32))
            + state.astype(jnp.float32)
        ).astype(jnp.bfloat16)
    squeezed = jnp.dot(
        state,
        lax.all_gather(comp_weight[0], "shard", axis=0, tiled=True),
        preferred_element_type=jnp.float32,
    )
    squeezed = (squeezed + comp_bias[0].astype(jnp.float32)).astype(jnp.bfloat16)
    tower_rows = lax.all_gather(over_weight, "shard", axis=1, tiled=True)
    summed = lax.psum_scatter(
        jnp.dot(squeezed, tower_rows, preferred_element_type=jnp.float32).astype(jnp.bfloat16),
        "tower",
        scatter_dimension=0,
        tiled=True,
    ).astype(jnp.float32)
    result = jax.nn.relu(summed + over_bias.astype(jnp.float32)).astype(jnp.bfloat16)
    return result.reshape(1, result.shape[0], result.shape[1])


def make_kernel(n, layers, tables_each, slot_most, n_devices):
    weights = 2 * layers + 1

    def kernel(
        wanted, pooled, down, up, comp, over, bias_in, over_bias, out,
        down_all, up_all, comp_all, over_all, cross_hop, comp_hop, pool_hop, received, base, state, total, lowered,
        squeezed, joined, bias, bias_wide,
        hop_send, hop_recv, first_send, first_recv, second_send, second_recv, core_send, core_recv,
        over_send, over_recv, pool_hop_send, pool_hop_recv, pool_send, pool_recv, mix_send, mix_recv, bias_send, bias_recv,
    ):
        t = lax.axis_index("tower")
        shard = lax.axis_index("shard")
        z, c = shard // CORES, shard % CORES
        other = 1 - c
        partner = (t, z * CORES + other)
        n_shard = n * CORES

        def remote(src, dst, send, recv, device):
            return pltpu.make_async_remote_copy(
                src_ref=src, dst_ref=dst, send_sem=send, recv_sem=recv,
                device_id=device, device_id_type=MESH,
            )

        barrier = pltpu.get_barrier_semaphore()
        mine = t * n_shard + shard

        @pl.loop(0, n_devices)
        def _(index):
            @pl.when(index != mine)
            def _():
                pl.semaphore_signal(
                    barrier, inc=1, device_id=(index // n_shard, index % n_shard), device_id_type=MESH
                )

        pl.semaphore_wait(barrier, n_devices - 1)

        pairs = []
        for layer in range(layers):
            pairs.append((down.at[layer], down_all.at[layer]))
            pairs.append((up.at[layer], up_all.at[layer]))
        pairs.append((comp, comp_all))

        def part(i, core, q):
            return over_all.at[q, :, core] if i == weights else pairs[i][1].at[:, core, q]

        def turn(k):
            return lax.rem(t + k, n)

        @pl.when(t == z)
        def _():
            local = pltpu.make_async_copy(bias_in, bias, bias_recv.at[0])
            local.start()
            for k in range(1, n):
                remote(bias_in, bias, bias_send.at[k], bias_recv.at[0], (turn(k), shard)).start()
            local.wait()

        def hop_of(i):
            return comp_hop if i == weights - 1 else cross_hop.at[i]

        def hop_copy(i, k):
            q = turn(k)
            return remote(
                pairs[i][0].at[q], hop_of(i).at[t], hop_send.at[i, k], hop_recv.at[i, t], (q, shard)
            )

        def hop_wait(i, k):
            tower = turn(k)
            view = hop_of(i).at[tower]
            remote(view, view, hop_send.at[i, k], hop_recv.at[i, tower], (t, shard)).wait_recv()

        def first_source(i, k):
            return pairs[i][0].at[t] if k == 0 else hop_of(i).at[turn(k)]

        def first_copy(i, k):
            return remote(
                first_source(i, k), pairs[i][1].at[z, c, t], first_send.at[i, k], first_recv.at[i, z],
                (t, turn(k) * CORES + c),
            )

        def first_local(i, k):
            return pltpu.make_async_copy(first_source(i, k), pairs[i][1].at[z, c, t], first_recv.at[i, z])

        def first_start(i, k):
            here = turn(k) == z

            @pl.when(here)
            def _():
                first_local(i, k).start()

            @pl.when(jnp.logical_not(here))
            def _():
                first_copy(i, k).start()

        def first_wait(i):
            first_local(i, 0).wait()
            for k in range(1, n):
                source = lax.rem(z + k, n)
                view = pairs[i][1].at[source, c, t]
                remote(view, view, first_send.at[i, 0], first_recv.at[i, source], (t, shard)).wait_recv()

        def over_copy(k):
            there = lax.rem(z + k, n)
            return remote(
                over, over_all.at[t, z, c], over_send.at[k], over_recv.at[z], (t, there * CORES + c)
            )

        over_local = pltpu.make_async_copy(over, over_all.at[t, z, c], over_recv.at[z])

        def over_wait():
            over_local.wait()
            for k in range(1, n):
                source = lax.rem(z + k, n)
                view = over_all.at[t, source, c]
                remote(view, view, over_send.at[k], over_recv.at[source], (t, shard)).wait_recv()

        per = slot_most // CHUNKS

        def pool_hop_copy(h, k):
            q = turn(k)
            slots = pl.ds(h * per, per)
            return remote(
                pooled.at[slots, :, :, q], pool_hop.at[t, slots], pool_hop_send.at[h, k],
                pool_hop_recv.at[h, t], (q, shard),
            )

        def pool_hop_wait(h, k):
            tower = turn(k)
            view = pool_hop.at[tower, pl.ds(h * per, per)]
            remote(view, view, pool_hop_send.at[h, k], pool_hop_recv.at[h, tower], (t, shard)).wait_recv()

        def pool_source(h, k, core):
            slots = pl.ds(h * per, per)
            return pooled.at[slots, :, core, t] if k == 0 else pool_hop.at[turn(k), slots, :, core]

        def pool_copy(h, k, core):
            return remote(
                pool_source(h, k, core), received.at[shard, pl.ds(h * per, per)],
                pool_send.at[h, k, core], pool_recv.at[h, shard], (t, turn(k) * CORES + core),
            )

        def pool_local(h, k):
            return pltpu.make_async_copy(
                pool_source(h, k, c), received.at[shard, pl.ds(h * per, per)], pool_recv.at[h, shard]
            )

        def pool_start(h, k):
            for core in range(CORES):
                here = jnp.logical_and(turn(k) == z, c == core)

                @pl.when(here)
                def _():
                    pool_local(h, k).start()

                @pl.when(jnp.logical_not(here))
                def _():
                    pool_copy(h, k, core).start()

        def pool_wait(h):
            pool_local(h, 0).wait()
            for k in range(1, n_shard):
                source = lax.rem(shard + k, n_shard)
                view = received.at[source, pl.ds(h * per, per)]
                remote(view, view, pool_send.at[h, 0, 0], pool_recv.at[h, source], (t, shard)).wait_recv()

        across, along = t % SIDE, t // SIDE
        x_next = along * SIDE + (1 - across)
        y_next = (1 - along) * SIDE + across
        diagonal = (1 - along) * SIDE + (1 - across)
        near = (t, x_next, y_next, diagonal)
        half = n // 2
        halves = (pl.ds(0, half), pl.ds(half, half))

        def second_copy(i, k):
            if k < 2:
                view = part(i, c, t)
                target = near[1 + k]
            else:
                view = part(i, c, near[k - 1]).at[halves[k - 2]]
                target = near[4 - k]
            return remote(view, view, second_send.at[i, k], second_recv.at[i, k], (target, shard))

        def second_wait(i, k):
            view = part(i, c, near[1 + k]) if k < 2 else part(i, c, diagonal).at[halves[k - 2]]
            remote(view, view, second_send.at[i, k], second_recv.at[i, k], (t, shard)).wait_recv()

        def core_copy(i, k):
            view = part(i, c, near[k])
            return remote(view, view, core_send.at[i, k], core_recv.at[i, k], partner)

        def second_start(i):
            second_copy(i, 0).start()
            second_copy(i, 1).start()
            core_copy(i, 0).start()

        def relay(i):
            for k in range(2):
                second_wait(i, k)
                second_copy(i, 2 + k).start()
                core_copy(i, 1 + k).start()

        def last(i):
            second_wait(i, 2)
            second_wait(i, 3)
            core_copy(i, 3).start()

        def complete(i):
            for k in range(n):
                view = part(i, other, near[k])
                remote(view, view, core_send.at[i, k], core_recv.at[i, k], partner).wait_recv()

        def hop_start(i):
            for k in range(1, n):
                hop_copy(i, k).start()

        def pool_hop_start(h):
            for k in range(1, n):
                pool_hop_copy(h, k).start()

        def hop_on(i):
            for k in range(1, n):
                hop_wait(i, k)
                first_start(i, k)

        def pool_on(h):
            for k in range(1, n):
                pool_hop_wait(h, k)
                pool_start(h, k)

        def spread(i):
            first_wait(i)
            second_start(i)

        early = 2
        for i in range(early):
            hop_start(i)
        pool_hop_start(0)
        for i in range(early, weights):
            hop_start(i)
        for h in range(1, CHUNKS):
            pool_hop_start(h)
        for i in range(early):
            first_start(i, 0)
        pool_start(0, 0)
        for i in range(early):
            hop_on(i)
        for i in range(early, weights):
            first_start(i, 0)
        over_local.start()
        for k in range(1, n):
            over_copy(k).start()
        pool_on(0)
        for h in range(1, CHUNKS):
            pool_start(h, 0)
        for i in range(early, weights):
            hop_on(i)
        for i in range(early):
            spread(i)
        for h in range(1, CHUNKS):
            pool_on(h)
        for i in range(early, weights):
            spread(i)
            relay(i - early)
        over_wait()
        second_start(weights)
        for i in range(weights - early, weights):
            last(i - weights + early)
            relay(i)
        last(early)

        @pl.when(t != z)
        def _():
            remote(bias, bias, bias_send.at[0], bias_recv.at[0], (t, shard)).wait_recv()

        bias_wide[...] = bias[...].astype(F32)
        for h in range(CHUNKS):
            pool_wait(h)

        rows = base.shape[1]
        width = base.shape[2]
        emb = width // tables_each
        blocks = base.shape[0]

        @pl.loop(0, blocks)
        def _(s):
            for k in range(tables_each):
                slot = wanted[s * tables_each + k]
                base[s, :, k * emb:(k + 1) * emb] = received[slot // slot_most, slot % slot_most].reshape(rows, emb)

        for layer in range(layers):
            complete(2 * layer)
            current = base if layer == 0 else state
            total[...] = jnp.zeros_like(total)

            @pl.loop(0, blocks)
            def _(s):
                total[...] += jnp.dot(
                    current[s], down_all[layer, s // CORES, s % CORES].reshape(width, -1),
                    preferred_element_type=F32,
                )

            lowered[...] = total[...].astype(BF16)
            if layer == 0:
                relay(weights)
                for i in range(early + 1, weights):
                    last(i)
            complete(2 * layer + 1)

            @pl.loop(0, blocks)
            def _(s):
                raised = jnp.dot(
                    lowered[...], up_all[layer, s // CORES, s % CORES].reshape(lowered.shape[1], width),
                    preferred_element_type=F32,
                )
                for k in range(tables_each):
                    cols = slice(k * emb, (k + 1) * emb)
                    row = bias_wide[pl.ds((layer * blocks + s) * tables_each + k, 1), :]
                    state[s, :, cols] = (
                        base[s, :, cols].astype(F32) * (raised[:, cols] + row)
                        + current[s, :, cols].astype(F32)
                    ).astype(BF16)

        last(weights)
        complete(2 * layers)
        cmp = squeezed.shape[2]
        total[:, :cmp] = jnp.zeros((rows, cmp), F32)

        @pl.loop(0, blocks)
        def _(s):
            total[:, :cmp] += jnp.dot(
                state[s], comp_all[s // CORES, s % CORES].reshape(width, cmp), preferred_element_type=F32
            )

        first_row = layers * blocks * tables_each
        for k in range(cmp // emb):
            cols = slice(k * emb, (k + 1) * emb)
            row = bias_wide[first_row + k:first_row + k + 1, :]
            squeezed[:, :, cols] = (total[:, cols] + row).astype(BF16).reshape(n, rows // n, emb)

        def mix_copy(k):
            there = lax.rem(z + k, n)
            return remote(
                squeezed.at[there], joined.at[z], mix_send.at[k], mix_recv.at[z], (t, there * CORES + c)
            )

        mix_local = pltpu.make_async_copy(squeezed.at[z], joined.at[z], mix_recv.at[z])
        for k in range(1, n):
            mix_copy(k).start()
        mix_local.start()
        complete(weights)
        mix_local.wait()
        for k in range(1, n):
            source = lax.rem(z + k, n)
            view = joined.at[source]
            remote(view, view, mix_send.at[k], mix_recv.at[source], (t, shard)).wait_recv()
        wide = over_all.shape[4]
        for s in range(n_shard):
            mixed = over_bias[:, s * wide:(s + 1) * wide].astype(F32)
            for tower in range(n):
                mixed = mixed + jnp.dot(
                    joined[tower], over_all[tower, s // CORES, s % CORES], preferred_element_type=F32
                )
            out[:, s * wide:(s + 1) * wide] = jnp.maximum(mixed, 0.0).astype(BF16)

        for k in range(1, n):
            over_copy(k).wait_send()
            for h in range(CHUNKS):
                pool_hop_copy(h, k).wait_send()
        for i in range(weights):
            for k in range(1, n):
                hop_copy(i, k).wait_send()
        for k in range(n):
            @pl.when(turn(k) != z)
            def _():
                for i in range(weights):
                    first_copy(i, k).wait_send()

            for core in range(CORES):
                @pl.when(jnp.logical_or(turn(k) != z, c != core))
                def _():
                    for h in range(CHUNKS):
                        pool_copy(h, k, core).wait_send()
        for i in range(weights + 1):
            for k in range(4):
                second_copy(i, k).wait_send()
                core_copy(i, k).wait_send()
        for k in range(1, n):
            mix_copy(k).wait_send()

        @pl.when(t == z)
        def _():
            for k in range(1, n):
                remote(bias_in, bias, bias_send.at[k], bias_recv.at[0], (turn(k), shard)).wait_send()

    return kernel


def turned(
    pooled, cross_down, cross_up, cross_bias, comp_weight, comp_bias, over_weight, over_bias,
    table_tower, table_owner,
):
    n = lax.axis_size("tower")
    n_shard = lax.axis_size("shard")
    layer_id = lax.axis_index("shard") // CORES
    _, samples, slot_most, emb = pooled.shape
    layers, depth, rank = cross_down.shape[1:]
    width = cross_up.shape[3]
    cmp = comp_weight.shape[2]
    tables_each = width // emb
    per_tower = tables_each * n_shard
    block = samples // (n_shard * n)
    rows = n * block
    out_width = over_bias.shape[0]
    wanted = slot_order(table_tower, table_owner, layer_id, per_tower, slot_most)
    pool_view = jnp.transpose(pooled[0], (1, 0, 2)).reshape(slot_most, n, CORES, n, block, emb)
    down = cross_down[0].reshape(layers, n, depth // n, rank)
    up = cross_up[0].reshape(layers, n, rank // n, width)
    comp = comp_weight[0].reshape(n, depth // n, cmp)
    bias_rows = jnp.concatenate([cross_bias[0].reshape(-1, emb), comp_bias[0].reshape(-1, emb)], axis=0)
    bias_rows = jnp.pad(bias_rows, ((0, -bias_rows.shape[0] % 16), (0, 0)))
    weights = 2 * layers + 1
    dma = pltpu.SemaphoreType.DMA
    any_spec = pl.BlockSpec(memory_space=pl.ANY)
    vmem_spec = pl.BlockSpec(memory_space=pltpu.VMEM)
    result = pl.pallas_call(
        make_kernel(n, layers, tables_each, slot_most, n * n_shard),
        out_shape=jax.ShapeDtypeStruct((block, out_width), BF16),
        in_specs=[pl.BlockSpec(memory_space=pltpu.SMEM)] + [any_spec] * 6 + [vmem_spec],
        out_specs=vmem_spec,
        scratch_shapes=[
            pltpu.VMEM((layers, n, CORES, n, depth // n, rank), BF16),
            pltpu.VMEM((layers, n, CORES, n, rank // n, width), BF16),
            pltpu.VMEM((n, CORES, n, depth // n, cmp), BF16),
            pltpu.VMEM((n, n, CORES) + over_weight.shape, BF16),
            pltpu.VMEM((2 * layers, n, depth // n, rank), BF16),
            pltpu.VMEM((n, depth // n, cmp), BF16),
            pltpu.VMEM((n, slot_most, n, CORES, block, emb), BF16),
            pltpu.VMEM((n_shard, slot_most, n, block, emb), BF16),
            pltpu.VMEM((n_shard, rows, width), BF16),
            pltpu.VMEM((n_shard, rows, width), BF16),
            pltpu.VMEM((rows, rank), F32),
            pltpu.VMEM((rows, rank), BF16),
            pltpu.VMEM((n, block, cmp), BF16),
            pltpu.VMEM((n, block, cmp), BF16),
            pltpu.VMEM(bias_rows.shape, BF16),
            pltpu.VMEM(bias_rows.shape, F32),
            dma((weights, n)), dma((weights, n)),
            dma((weights, n)), dma((weights, n)),
            dma((weights + 1, n)), dma((weights + 1, n)),
            dma((weights + 1, n)), dma((weights + 1, n)),
            dma((n,)), dma((n,)),
            dma((CHUNKS, n)), dma((CHUNKS, n)),
            dma((CHUNKS, n, CORES)), dma((CHUNKS, n_shard)),
            dma((n,)), dma((n,)),
            dma((n,)), dma((1,)),
        ],
        compiler_params=pltpu.CompilerParams(
            collective_id=0, has_side_effects=True, vmem_limit_bytes=60 * 1024 * 1024
        ),
        name="towers",
    )(wanted, pool_view, down, up, comp, over_weight, bias_rows, over_bias.reshape(1, -1))
    return result.reshape(1, block, out_width)


def solution(mesh):
    placed = (
        P("tower", None, "shard", None),
        P("tower", None, "shard", None),
        P("tower", None, None, "shard"),
        P("tower", None, None),
        P("tower", "shard", None),
        P("tower", None),
        P("tower", "shard"),
        P(),
        P(),
        P(),
    )
    towers, shards = mesh.shape["tower"], mesh.shape["shard"]
    body = turned if towers == SIDE * SIDE and towers * CORES == shards else on_device
    return jax.shard_map(
        body, mesh=mesh, in_specs=placed, out_specs=P("shard", "tower", None), check_vma=False
    )
```

profile of v0, /device:TPU:1, one launch (start us, length us, event | category | flops | bytes accessed | tf_op | source)
XLA Modules:
  0.0 227.9 jit_solution(318840297596340072)
XLA Ops:
  0.0 0.7 broadcast_compare_fusion
  0.7 0.7 reduce
  1.4 0.9 convert_reduce_fusion.1
  2.3 0.7 multiply_add_fusion
  2.9 0.7 select_reduce_fusion.wanted
  3.6 1.3 reshape.15.over_bias
  4.9 0.7 reshape_squeeze.18
  5.6 0.6 fusion.4.bias_in
  6.2 220.0 %towers.1 = bf16[96,1024]{1,0:T(8,128)(2,1)} custom-call(s32[32]{0:T(128)} %select_reduce_fusion.wanted, bf16[6,4,2,4,96,128]{5,4,3,2,1,0:T(8,128)(2,1)} %bitcast.10, bf16[2,4,128,512]{3,2,1,0:T(8,128)(2,1)} %bitcast.11, bf16[2,4,128,512]{3,2,1,0:T(8,128)(2,1)} %bitcast.12, bf16[4,128,256]{2,1,0:T(8,128)(2,1)} %bitcast.14, bf16[256,128]{1,0:T(8,128)(2,1)} %over.1, ...), custom_call_target="tpu_custom_call" | custom-call | tf_op jit(solution)/shard_map/towers/pallas_call | solution.py:510
  226.3 1.6 copy.12
where the time goes:
time: 232 us; the launch traced here: 228 us
  Pallas kernels  220 us (95%)
  other arithmetic  4.19 us (2%)
  local copies, waits for them, and re-layouts  3.62 us (2%)
    pallas_call x1, Pallas kernels, turned(): pl.pallas_call(make_kernel(n, layers, tables_each, slot_most, n * n_shard...  220 us

commit v1 on v0

--- a/solution.py
+++ b/solution.py
@@ -47,7 +47,9 @@
     per_tower = feature_count // emb_width
     received = lax.all_to_all(pooled, "shard", split_axis=1, concat_axis=2, tiled=True)
     wanted = slot_order(table_tower, table_owner, tower_id, per_tower, slot_most)
-    tables = jnp.take(received[0], wanted, axis=1)
+    tables = jnp.concatenate(
+        [lax.dynamic_slice_in_dim(received[0], wanted[k], 1, axis=1) for k in range(per_tower)], axis=1
+    )
     sample_count = tables.shape[0]
     base = tables.reshape(sample_count, feature_count)
     state = base
@@ -316,42 +318,48 @@
             first_wait(i)
             second_start(i)
 
-        early = 2
-        for i in range(early):
+        ahead = 3
+        for i in range(weights):
             hop_start(i)
         pool_hop_start(0)
-        for i in range(early, weights):
-            hop_start(i)
-        for h in range(1, CHUNKS):
-            pool_hop_start(h)
-        for i in range(early):
+        for i in range(ahead):
             first_start(i, 0)
-        pool_start(0, 0)
-        for i in range(early):
+        for i in range(ahead):
             hop_on(i)
-        for i in range(early, weights):
+        spread(0)
+        pool_hop_start(1)
+        for i in range(ahead, weights):
             first_start(i, 0)
+            hop_on(i)
         over_local.start()
         for k in range(1, n):
             over_copy(k).start()
+        for h in range(CHUNKS):
+            pool_start(h, 0)
+        spread(1)
+        pool_hop_start(2)
         pool_on(0)
-        for h in range(1, CHUNKS):
-            pool_start(h, 0)
-        for i in range(early, weights):
-            hop_on(i)
-        for i in range(early):
-            spread(i)
-        for h in range(1, CHUNKS):
-            pool_on(h)
-        for i in range(early, weights):
-            spread(i)
-            relay(i - early)
+        spread(2)
+        pool_hop_start(3)
+        spread(3)
+        pool_hop_start(4)
+        pool_on(1)
+        spread(4)
+        pool_hop_start(5)
         over_wait()
         second_start(weights)
-        for i in range(weights - early, weights):
-            last(i - weights + early)
-            relay(i)
-        last(early)
+        relay(0)
+        pool_on(2)
+        relay(1)
+        pool_on(3)
+        relay(2)
+        pool_on(4)
+        relay(3)
+        pool_on(5)
+        relay(4)
+        relay(weights)
+        for i in range(weights):
+            last(i)
 
         @pl.when(t != z)
         def _():
@@ -385,10 +393,6 @@
                 )
 
             lowered[...] = total[...].astype(BF16)
-            if layer == 0:
-                relay(weights)
-                for i in range(early + 1, weights):
-                    last(i)
             complete(2 * layer + 1)
 
             @pl.loop(0, blocks)

time: 232 us -> 212 us (0.914); the launches traced: 228 us -> 211 us
  Pallas kernels: 220 us -> 203 us
    pallas_call x1, Pallas kernels: 220 us -> 203 us  [turned(): pl.pallas_call(make_kernel(n, layers, tables_each, slot_most, n * n_shard...]
where the time goes in v1:
time: 212 us; the launch traced here: 211 us
  Pallas kernels  203 us (96%)
  other arithmetic  4.19 us (2%)
  local copies, waits for them, and re-layouts  3.62 us (2%)
    pallas_call x1, Pallas kernels, turned(): pl.pallas_call(make_kernel(n, layers, tables_each, slot_most, n * n_shard...  203 us

profile of v1, /device:TPU:1, one launch (start us, length us, event | category | flops | bytes accessed | tf_op | source)
XLA Modules:
  0.0 211.2 jit_solution(13108901097707049072)
XLA Ops:
  0.0 0.7 broadcast_compare_fusion
  0.7 0.7 reduce
  1.4 0.9 convert_reduce_fusion.1
  2.3 0.7 multiply_add_fusion
  2.9 0.7 select_reduce_fusion.wanted
  3.6 1.3 reshape.15.over_bias
  4.9 0.7 reshape_squeeze.18
  5.6 0.6 fusion.4.bias_in
  6.2 203.4 %towers.1 = bf16[96,1024]{1,0:T(8,128)(2,1)} custom-call(s32[32]{0:T(128)} %select_reduce_fusion.wanted, bf16[6,4,2,4,96,128]{5,4,3,2,1,0:T(8,128)(2,1)} %bitcast.10, bf16[2,4,128,512]{3,2,1,0:T(8,128)(2,1)} %bitcast.11, bf16[2,4,128,512]{3,2,1,0:T(8,128)(2,1)} %bitcast.12, bf16[4,128,256]{2,1,0:T(8,128)(2,1)} %bitcast.14, bf16[256,128]{1,0:T(8,128)(2,1)} %over.1, ...), custom_call_target="tpu_custom_call" | custom-call | tf_op jit(solution)/shard_map/towers/pallas_call | solution.py:514
  209.6 1.6 copy.12

commit v2 on v1

--- a/solution.py
+++ b/solution.py
@@ -8,7 +8,6 @@
 MESH = pl.DeviceIdType.MESH
 CORES = 2
 SIDE = 2
-CHUNKS = 6
 BF16, F32 = jnp.bfloat16, jnp.float32
 
 
@@ -86,12 +85,12 @@
     return result.reshape(1, result.shape[0], result.shape[1])
 
 
-def make_kernel(n, layers, tables_each, slot_most, n_devices):
+def make_kernel(n, layers, tables_each, slot_most):
     weights = 2 * layers + 1
 
     def kernel(
         wanted, pooled, down, up, comp, over, bias_in, over_bias, out,
-        down_all, up_all, comp_all, over_all, cross_hop, comp_hop, pool_hop, received, base, state, total, lowered,
+        down_all, up_all, comp_all, over_all, cross_hop, comp_hop, pool_hop, received, received_last, base, state, total, lowered,
         squeezed, joined, bias, bias_wide,
         hop_send, hop_recv, first_send, first_recv, second_send, second_recv, core_send, core_recv,
         over_send, over_recv, pool_hop_send, pool_hop_recv, pool_send, pool_recv, mix_send, mix_recv, bias_send, bias_recv,
@@ -110,17 +109,11 @@
             )
 
         barrier = pltpu.get_barrier_semaphore()
-        mine = t * n_shard + shard
-
-        @pl.loop(0, n_devices)
-        def _(index):
-            @pl.when(index != mine)
-            def _():
-                pl.semaphore_signal(
-                    barrier, inc=1, device_id=(index // n_shard, index % n_shard), device_id_type=MESH
-                )
-
-        pl.semaphore_wait(barrier, n_devices - 1)
+        for k in range(1, n):
+            pl.semaphore_signal(barrier, inc=1, device_id=(lax.rem(t + k, n), shard), device_id_type=MESH)
+        for k in range(1, n_shard):
+            pl.semaphore_signal(barrier, inc=1, device_id=(t, lax.rem(shard + k, n_shard)), device_id_type=MESH)
+        pl.semaphore_wait(barrier, n + n_shard - 2)
 
         pairs = []
         for layer in range(layers):
@@ -201,35 +194,31 @@
                 view = over_all.at[t, source, c]
                 remote(view, view, over_send.at[k], over_recv.at[source], (t, shard)).wait_recv()
 
-        per = slot_most // CHUNKS
-
         def pool_hop_copy(h, k):
             q = turn(k)
-            slots = pl.ds(h * per, per)
             return remote(
-                pooled.at[slots, :, :, q], pool_hop.at[t, slots], pool_hop_send.at[h, k],
-                pool_hop_recv.at[h, t], (q, shard),
+                pooled.at[:, h, :, q], pool_hop.at[t, :, h], pool_hop_send.at[h, k], pool_hop_recv.at[h, t], (q, shard)
             )
 
         def pool_hop_wait(h, k):
             tower = turn(k)
-            view = pool_hop.at[tower, pl.ds(h * per, per)]
+            view = pool_hop.at[tower, :, h]
             remote(view, view, pool_hop_send.at[h, k], pool_hop_recv.at[h, tower], (t, shard)).wait_recv()
 
         def pool_source(h, k, core):
-            slots = pl.ds(h * per, per)
-            return pooled.at[slots, :, core, t] if k == 0 else pool_hop.at[turn(k), slots, :, core]
+            return pooled.at[:, h, core, t] if k == 0 else pool_hop.at[turn(k), :, h, core]
+
+        def pool_place(h, owner):
+            return received.at[owner, :, h] if h < n - 1 else received_last.at[owner]
 
         def pool_copy(h, k, core):
             return remote(
-                pool_source(h, k, core), received.at[shard, pl.ds(h * per, per)],
-                pool_send.at[h, k, core], pool_recv.at[h, shard], (t, turn(k) * CORES + core),
+                pool_source(h, k, core), pool_place(h, shard), pool_send.at[h, k, core], pool_recv.at[h, shard],
+                (t, turn(k) * CORES + core),
             )
 
         def pool_local(h, k):
-            return pltpu.make_async_copy(
-                pool_source(h, k, c), received.at[shard, pl.ds(h * per, per)], pool_recv.at[h, shard]
-            )
+            return pltpu.make_async_copy(pool_source(h, k, c), pool_place(h, shard), pool_recv.at[h, shard])
 
         def pool_start(h, k):
             for core in range(CORES):
@@ -247,7 +236,7 @@
             pool_local(h, 0).wait()
             for k in range(1, n_shard):
                 source = lax.rem(shard + k, n_shard)
-                view = received.at[source, pl.ds(h * per, per)]
+                view = pool_place(h, source)
                 remote(view, view, pool_send.at[h, 0, 0], pool_recv.at[h, source], (t, shard)).wait_recv()
 
         across, along = t % SIDE, t // SIDE
@@ -318,130 +307,160 @@
             first_wait(i)
             second_start(i)
 
-        ahead = 3
-        for i in range(weights):
-            hop_start(i)
-        pool_hop_start(0)
-        for i in range(ahead):
-            first_start(i, 0)
-        for i in range(ahead):
-            hop_on(i)
-        spread(0)
-        pool_hop_start(1)
-        for i in range(ahead, weights):
-            first_start(i, 0)
-            hop_on(i)
-        over_local.start()
-        for k in range(1, n):
-            over_copy(k).start()
-        for h in range(CHUNKS):
-            pool_start(h, 0)
-        spread(1)
-        pool_hop_start(2)
-        pool_on(0)
-        spread(2)
-        pool_hop_start(3)
-        spread(3)
-        pool_hop_start(4)
-        pool_on(1)
-        spread(4)
-        pool_hop_start(5)
-        over_wait()
-        second_start(weights)
-        relay(0)
-        pool_on(2)
-        relay(1)
-        pool_on(3)
-        relay(2)
-        pool_on(4)
-        relay(3)
-        pool_on(5)
-        relay(4)
-        relay(weights)
-        for i in range(weights):
-            last(i)
-
-        @pl.when(t != z)
-        def _():
-            remote(bias, bias, bias_send.at[0], bias_recv.at[0], (t, shard)).wait_recv()
-
-        bias_wide[...] = bias[...].astype(F32)
-        for h in range(CHUNKS):
-            pool_wait(h)
-
         rows = base.shape[1]
         width = base.shape[2]
         emb = width // tables_each
         blocks = base.shape[0]
-
-        @pl.loop(0, blocks)
-        def _(s):
-            for k in range(tables_each):
-                slot = wanted[s * tables_each + k]
-                base[s, :, k * emb:(k + 1) * emb] = received[slot // slot_most, slot % slot_most].reshape(rows, emb)
-
-        for layer in range(layers):
-            complete(2 * layer)
-            current = base if layer == 0 else state
-            total[...] = jnp.zeros_like(total)
-
+        block = rows // n
+        cmp = squeezed.shape[2]
+
+        def gather(source, lo, hi):
             @pl.loop(0, blocks)
             def _(s):
-                total[...] += jnp.dot(
-                    current[s], down_all[layer, s // CORES, s % CORES].reshape(width, -1),
+                for k in range(tables_each):
+                    slot = wanted[s * tables_each + k]
+                    base[s, lo:hi, k * emb:(k + 1) * emb] = source[slot // slot_most, slot % slot_most].reshape(
+                        hi - lo, emb
+                    )
+
+        def lower(layer, lo, hi):
+            current = base if layer == 0 else state
+            total[lo:hi, :] = jnp.zeros((hi - lo, total.shape[1]), F32)
+
+            @pl.loop(0, blocks)
+            def _(s):
+                total[lo:hi, :] += jnp.dot(
+                    current[s, lo:hi, :], down_all[layer, s // CORES, s % CORES].reshape(width, -1),
                     preferred_element_type=F32,
                 )
 
-            lowered[...] = total[...].astype(BF16)
-            complete(2 * layer + 1)
+            lowered[lo:hi, :] = total[lo:hi, :].astype(BF16)
+
+        def cross(layer, lo, hi):
+            current = base if layer == 0 else state
 
             @pl.loop(0, blocks)
             def _(s):
                 raised = jnp.dot(
-                    lowered[...], up_all[layer, s // CORES, s % CORES].reshape(lowered.shape[1], width),
+                    lowered[lo:hi, :], up_all[layer, s // CORES, s % CORES].reshape(lowered.shape[1], width),
                     preferred_element_type=F32,
                 )
                 for k in range(tables_each):
                     cols = slice(k * emb, (k + 1) * emb)
                     row = bias_wide[pl.ds((layer * blocks + s) * tables_each + k, 1), :]
-                    state[s, :, cols] = (
-                        base[s, :, cols].astype(F32) * (raised[:, cols] + row)
-                        + current[s, :, cols].astype(F32)
+                    state[s, lo:hi, cols] = (
+                        base[s, lo:hi, cols].astype(F32) * (raised[:, cols] + row)
+                        + current[s, lo:hi, cols].astype(F32)
                     ).astype(BF16)
 
-        last(weights)
-        complete(2 * layers)
-        cmp = squeezed.shape[2]
-        total[:, :cmp] = jnp.zeros((rows, cmp), F32)
-
-        @pl.loop(0, blocks)
-        def _(s):
-            total[:, :cmp] += jnp.dot(
-                state[s], comp_all[s // CORES, s % CORES].reshape(width, cmp), preferred_element_type=F32
-            )
-
-        first_row = layers * blocks * tables_each
-        for k in range(cmp // emb):
-            cols = slice(k * emb, (k + 1) * emb)
-            row = bias_wide[first_row + k:first_row + k + 1, :]
-            squeezed[:, :, cols] = (total[:, cols] + row).astype(BF16).reshape(n, rows // n, emb)
-
-        def mix_copy(k):
-            there = lax.rem(z + k, n)
+        def mix_copy(there):
             return remote(
-                squeezed.at[there], joined.at[z], mix_send.at[k], mix_recv.at[z], (t, there * CORES + c)
+                squeezed.at[there], joined.at[z], mix_send.at[there], mix_recv.at[z], (t, there * CORES + c)
             )
 
         mix_local = pltpu.make_async_copy(squeezed.at[z], joined.at[z], mix_recv.at[z])
+
+        def squeeze(lo, hi):
+            total[lo:hi, :cmp] = jnp.zeros((hi - lo, cmp), F32)
+
+            @pl.loop(0, blocks)
+            def _(s):
+                total[lo:hi, :cmp] += jnp.dot(
+                    state[s, lo:hi, :], comp_all[s // CORES, s % CORES].reshape(width, cmp), preferred_element_type=F32
+                )
+
+            first_row = layers * blocks * tables_each
+            for k in range(cmp // emb):
+                cols = slice(k * emb, (k + 1) * emb)
+                row = bias_wide[first_row + k:first_row + k + 1, :]
+                squeezed[lo // block:hi // block, :, cols] = (
+                    (total[lo:hi, cols] + row).astype(BF16).reshape((hi - lo) // block, block, emb)
+                )
+            for there in range(lo // block, hi // block):
+                @pl.when(z == there)
+                def _():
+                    mix_local.start()
+
+                @pl.when(z != there)
+                def _():
+                    mix_copy(there).start()
+
+        comp_id, over_id = weights - 1, weights
+        hop_start(comp_id)
+        for i in range(comp_id):
+            hop_start(i)
+        pool_hop_start(0)
+        for i in (comp_id, 0, 1):
+            first_start(i, 0)
+        for i in (comp_id, 0, 1):
+            hop_on(i)
+        spread(comp_id)
+        first_start(2, 0)
+        hop_on(2)
+        spread(0)
+        first_start(3, 0)
+        hop_on(3)
+        over_local.start()
         for k in range(1, n):
-            mix_copy(k).start()
-        mix_local.start()
-        complete(weights)
+            over_copy(k).start()
+        for h in range(n):
+            pool_start(h, 0)
+        spread(1)
+        pool_hop_start(1)
+        pool_on(0)
+        spread(2)
+        pool_hop_start(2)
+        spread(3)
+        relay(comp_id)
+        pool_on(1)
+        relay(0)
+        relay(1)
+        pool_hop_start(3)
+        pool_on(2)
+        relay(2)
+        relay(3)
+        over_wait()
+        second_start(over_id)
+        pool_on(3)
+        last(comp_id)
+        last(0)
+
+        @pl.when(t != z)
+        def _():
+            remote(bias, bias, bias_send.at[0], bias_recv.at[0], (t, shard)).wait_recv()
+
+        bias_wide[...] = bias[...].astype(F32)
+        for h in range(n - 1):
+            pool_wait(h)
+        early, late = (0, rows - block), (rows - block, rows)
+        gather(received, *early)
+        complete(0)
+        lower(0, *early)
+        last(1)
+        complete(1)
+        cross(0, *early)
+        last(2)
+        complete(2)
+        lower(1, *early)
+        relay(over_id)
+        last(3)
+        complete(3)
+        cross(1, *early)
+        complete(comp_id)
+        squeeze(*early)
+        last(over_id)
+        pool_wait(n - 1)
+        gather(received_last, *late)
+        for layer in range(layers):
+            lower(layer, *late)
+            cross(layer, *late)
+        squeeze(*late)
+        complete(over_id)
         mix_local.wait()
         for k in range(1, n):
             source = lax.rem(z + k, n)
             view = joined.at[source]
-            remote(view, view, mix_send.at[k], mix_recv.at[source], (t, shard)).wait_recv()
+            remote(view, view, mix_send.at[0], mix_recv.at[source], (t, shard)).wait_recv()
         wide = over_all.shape[4]
         for s in range(n_shard):
             mixed = over_bias[:, s * wide:(s + 1) * wide].astype(F32)
@@ -453,7 +472,7 @@
 
         for k in range(1, n):
             over_copy(k).wait_send()
-            for h in range(CHUNKS):
+            for h in range(n):
                 pool_hop_copy(h, k).wait_send()
         for i in range(weights):
             for k in range(1, n):
@@ -467,14 +486,16 @@
             for core in range(CORES):
                 @pl.when(jnp.logical_or(turn(k) != z, c != core))
                 def _():
-                    for h in range(CHUNKS):
+                    for h in range(n):
                         pool_copy(h, k, core).wait_send()
         for i in range(weights + 1):
             for k in range(4):
                 second_copy(i, k).wait_send()
                 core_copy(i, k).wait_send()
-        for k in range(1, n):
-            mix_copy(k).wait_send()
+        for there in range(n):
+            @pl.when(z != there)
+            def _():
+                mix_copy(there).wait_send()
 
         @pl.when(t == z)
         def _():
@@ -512,7 +533,7 @@
     any_spec = pl.BlockSpec(memory_space=pl.ANY)
     vmem_spec = pl.BlockSpec(memory_space=pltpu.VMEM)
     result = pl.pallas_call(
-        make_kernel(n, layers, tables_each, slot_most, n * n_shard),
+        make_kernel(n, layers, tables_each, slot_most),
         out_shape=jax.ShapeDtypeStruct((block, out_width), BF16),
         in_specs=[pl.BlockSpec(memory_space=pltpu.SMEM)] + [any_spec] * 6 + [vmem_spec],
         out_specs=vmem_spec,
@@ -524,7 +545,8 @@
             pltpu.VMEM((2 * layers, n, depth // n, rank), BF16),
             pltpu.VMEM((n, depth // n, cmp), BF16),
             pltpu.VMEM((n, slot_most, n, CORES, block, emb), BF16),
-            pltpu.VMEM((n_shard, slot_most, n, block, emb), BF16),
+            pltpu.VMEM((n_shard, slot_most, n - 1, block, emb), BF16),
+            pltpu.VMEM((n_shard, slot_most, block, emb), BF16),
             pltpu.VMEM((n_shard, rows, width), BF16),
             pltpu.VMEM((n_shard, rows, width), BF16),
             pltpu.VMEM((rows, rank), F32),
@@ -538,8 +560,8 @@
             dma((weights + 1, n)), dma((weights + 1, n)),
             dma((weights + 1, n)), dma((weights + 1, n)),
             dma((n,)), dma((n,)),
-            dma((CHUNKS, n)), dma((CHUNKS, n)),
-            dma((CHUNKS, n, CORES)), dma((CHUNKS, n_shard)),
+            dma((n, n)), dma((n, n)),
+            dma((n, n, CORES)), dma((n, n_shard)),
             dma((n,)), dma((n,)),
             dma((n,)), dma((1,)),
         ],

time: 212 us -> 203 us (0.958)
  the two profiles are of different devices: /device:TPU:1 before, /device:TPU:30 now
where the time goes in v2:
time: 203 us
  Pallas kernels  195 us (96%)
  other arithmetic  4.19 us (2%)
  local copies, waits for them, and re-layouts  3.62 us (2%)
    pallas_call x1, Pallas kernels, turned(): pl.pallas_call(make_kernel(n, layers, tables_each, slot_most), out_shape=...  195 us

profile of v2, /device:TPU:30, one launch (start us, length us, event | category | flops | bytes accessed | tf_op | source)
XLA Modules:
  0.0 202.7 jit_solution(671326834294911310)
XLA Ops:
  0.0 0.7 broadcast_compare_fusion
  0.7 0.7 reduce
  1.4 0.9 convert_reduce_fusion.1
  2.3 0.7 multiply_add_fusion
  2.9 0.7 select_reduce_fusion.wanted
  3.6 1.3 reshape.15.over_bias
  4.9 0.7 reshape_squeeze.18
  5.6 0.6 fusion.4.bias_in
  6.2 194.9 %towers.1 = bf16[96,1024]{1,0:T(8,128)(2,1)} custom-call(s32[32]{0:T(128)} %select_reduce_fusion.wanted, bf16[6,4,2,4,96,128]{5,4,3,2,1,0:T(8,128)(2,1)} %bitcast.10, bf16[2,4,128,512]{3,2,1,0:T(8,128)(2,1)} %bitcast.11, bf16[2,4,128,512]{3,2,1,0:T(8,128)(2,1)} %bitcast.12, bf16[4,128,256]{2,1,0:T(8,128)(2,1)} %bitcast.14, bf16[256,128]{1,0:T(8,128)(2,1)} %over.1, ...), custom_call_target="tpu_custom_call" | custom-call | tf_op jit(solution)/shard_map/towers/pallas_call | solution.py:535
  201.1 1.6 copy.12

commit v3 on v2

--- a/solution.py
+++ b/solution.py
@@ -89,9 +89,9 @@
     weights = 2 * layers + 1
 
     def kernel(
-        wanted, pooled, down, up, comp, over, bias_in, over_bias, out,
+        table_tower, table_owner, pooled, down, up, comp, over, cross_bias, comp_bias, over_bias, out,
         down_all, up_all, comp_all, over_all, cross_hop, comp_hop, pool_hop, received, received_last, base, state, total, lowered,
-        squeezed, joined, bias, bias_wide,
+        squeezed, joined, bias, bias_low, bias_wide, order_row, wanted, order_sem,
         hop_send, hop_recv, first_send, first_recv, second_send, second_recv, core_send, core_recv,
         over_send, over_recv, pool_hop_send, pool_hop_recv, pool_send, pool_recv, mix_send, mix_recv, bias_send, bias_recv,
     ):
@@ -127,13 +127,34 @@
         def turn(k):
             return lax.rem(t + k, n)
 
+        biases = ((cross_bias, bias), (comp_bias, bias_low))
+
         @pl.when(t == z)
         def _():
-            local = pltpu.make_async_copy(bias_in, bias, bias_recv.at[0])
-            local.start()
-            for k in range(1, n):
-                remote(bias_in, bias, bias_send.at[k], bias_recv.at[0], (turn(k), shard)).start()
-            local.wait()
+            for i, (source, place) in enumerate(biases):
+                pltpu.make_async_copy(source, place, bias_recv.at[i]).start()
+                for k in range(1, n):
+                    remote(source, place, bias_send.at[i, k], bias_recv.at[i], (turn(k), shard)).start()
+
+        def order_tables():
+            count = table_tower.shape[0]
+            rows_of = lax.broadcasted_iota(jnp.int32, (count, count), 0)
+            cols_of = lax.broadcasted_iota(jnp.int32, (count, count), 1)
+
+            def column(row):
+                return jnp.sum(jnp.where(rows_of == cols_of, row, 0), axis=1, keepdims=True)
+
+            owner = table_owner[...].reshape(1, count)
+            inside = (table_tower[...].reshape(1, count) == z).astype(jnp.int32)
+            before = jnp.where(rows_of < cols_of, column(inside), 0)
+            position = jnp.sum(before, axis=0, keepdims=True)
+            own_slot = jnp.sum(jnp.where(column(owner) == owner, before, 0), axis=0, keepdims=True)
+            slot = owner * slot_most + own_slot
+            place = jnp.where(inside == 1, position, count)
+            order_row[...] = jnp.sum(
+                jnp.where(column(place) == cols_of, column(slot), 0), axis=0, keepdims=True
+            )
+            pltpu.make_async_copy(order_row, wanted, order_sem.at[0]).start()
 
         def hop_of(i):
             return comp_hop if i == weights - 1 else cross_hop.at[i]
@@ -197,7 +218,7 @@
         def pool_hop_copy(h, k):
             q = turn(k)
             return remote(
-                pooled.at[:, h, :, q], pool_hop.at[t, :, h], pool_hop_send.at[h, k], pool_hop_recv.at[h, t], (q, shard)
+                pooled.at[:, turn(1 + h), :, q], pool_hop.at[t, :, h], pool_hop_send.at[h, k], pool_hop_recv.at[h, t], (q, shard)
             )
 
         def pool_hop_wait(h, k):
@@ -206,7 +227,7 @@
             remote(view, view, pool_hop_send.at[h, k], pool_hop_recv.at[h, tower], (t, shard)).wait_recv()
 
         def pool_source(h, k, core):
-            return pooled.at[:, h, core, t] if k == 0 else pool_hop.at[turn(k), :, h, core]
+            return pooled.at[:, turn(1 + h), core, t] if k == 0 else pool_hop.at[turn(k), :, h, core]
 
         def pool_place(h, owner):
             return received.at[owner, :, h] if h < n - 1 else received_last.at[owner]
@@ -315,31 +336,40 @@
         cmp = squeezed.shape[2]
 
         def gather(source, lo, hi):
-            @pl.loop(0, blocks)
+            @pl.loop(0, blocks, unroll=True)
             def _(s):
                 for k in range(tables_each):
-                    slot = wanted[s * tables_each + k]
+                    slot = wanted[0, s * tables_each + k]
                     base[s, lo:hi, k * emb:(k + 1) * emb] = source[slot // slot_most, slot % slot_most].reshape(
                         hi - lo, emb
                     )
 
         def lower(layer, lo, hi):
             current = base if layer == 0 else state
-            total[lo:hi, :] = jnp.zeros((hi - lo, total.shape[1]), F32)
-
-            @pl.loop(0, blocks)
-            def _(s):
-                total[lo:hi, :] += jnp.dot(
-                    current[s, lo:hi, :], down_all[layer, s // CORES, s % CORES].reshape(width, -1),
-                    preferred_element_type=F32,
-                )
-
-            lowered[lo:hi, :] = total[lo:hi, :].astype(BF16)
+            if hi - lo > rows:
+                total[lo:hi, :] = jnp.zeros((hi - lo, total.shape[1]), F32)
+
+                @pl.loop(0, blocks)
+                def _(s):
+                    total[lo:hi, :] += jnp.dot(
+                        current[s, lo:hi, :], down_all[layer, s // CORES, s % CORES].reshape(width, -1),
+                        preferred_element_type=F32,
+                    )
+
+                lowered[lo:hi, :] = total[lo:hi, :].astype(BF16)
+            else:
+                added = jnp.zeros((hi - lo, total.shape[1]), F32)
+                for s in range(blocks):
+                    added = added + jnp.dot(
+                        current[s, lo:hi, :], down_all[layer, s // CORES, s % CORES].reshape(width, -1),
+                        preferred_element_type=F32,
+                    )
+                lowered[lo:hi, :] = added.astype(BF16)
 
         def cross(layer, lo, hi):
             current = base if layer == 0 else state
 
-            @pl.loop(0, blocks)
+            @pl.loop(0, blocks, unroll=True)
             def _(s):
                 raised = jnp.dot(
                     lowered[lo:hi, :], up_all[layer, s // CORES, s % CORES].reshape(lowered.shape[1], width),
@@ -347,43 +377,28 @@
                 )
                 for k in range(tables_each):
                     cols = slice(k * emb, (k + 1) * emb)
-                    row = bias_wide[pl.ds((layer * blocks + s) * tables_each + k, 1), :]
+                    row = bias_wide[layer:layer + 1, pl.ds(pl.multiple_of((s * tables_each + k) * emb, emb), emb)]
                     state[s, lo:hi, cols] = (
                         base[s, lo:hi, cols].astype(F32) * (raised[:, cols] + row)
                         + current[s, lo:hi, cols].astype(F32)
                     ).astype(BF16)
 
-        def mix_copy(there):
-            return remote(
-                squeezed.at[there], joined.at[z], mix_send.at[there], mix_recv.at[z], (t, there * CORES + c)
-            )
-
-        mix_local = pltpu.make_async_copy(squeezed.at[z], joined.at[z], mix_recv.at[z])
+        def mix_copy(h):
+            there = lax.rem(z + 1 + h, n)
+            return remote(squeezed.at[h], joined.at[z], mix_send.at[h], mix_recv.at[z], (t, there * CORES + c))
 
         def squeeze(lo, hi):
-            total[lo:hi, :cmp] = jnp.zeros((hi - lo, cmp), F32)
-
-            @pl.loop(0, blocks)
-            def _(s):
-                total[lo:hi, :cmp] += jnp.dot(
+            added = jnp.zeros((hi - lo, cmp), F32)
+            for s in range(blocks):
+                added = added + jnp.dot(
                     state[s, lo:hi, :], comp_all[s // CORES, s % CORES].reshape(width, cmp), preferred_element_type=F32
                 )
-
-            first_row = layers * blocks * tables_each
             for k in range(cmp // emb):
                 cols = slice(k * emb, (k + 1) * emb)
-                row = bias_wide[first_row + k:first_row + k + 1, :]
+                row = bias_low[:, cols].astype(F32)
                 squeezed[lo // block:hi // block, :, cols] = (
-                    (total[lo:hi, cols] + row).astype(BF16).reshape((hi - lo) // block, block, emb)
+                    (added[:, cols] + row).astype(BF16).reshape((hi - lo) // block, block, emb)
                 )
-            for there in range(lo // block, hi // block):
-                @pl.when(z == there)
-                def _():
-                    mix_local.start()
-
-                @pl.when(z != there)
-                def _():
-                    mix_copy(there).start()
 
         comp_id, over_id = weights - 1, weights
         hop_start(comp_id)
@@ -392,6 +407,7 @@
         pool_hop_start(0)
         for i in (comp_id, 0, 1):
             first_start(i, 0)
+        order_tables()
         for i in (comp_id, 0, 1):
             hop_on(i)
         spread(comp_id)
@@ -425,11 +441,17 @@
         last(comp_id)
         last(0)
 
-        @pl.when(t != z)
-        def _():
-            remote(bias, bias, bias_send.at[0], bias_recv.at[0], (t, shard)).wait_recv()
+        for i, (source, place) in enumerate(biases):
+            @pl.when(t == z)
+            def _():
+                pltpu.make_async_copy(source, place, bias_recv.at[i]).wait()
+
+            @pl.when(t != z)
+            def _():
+                remote(place, place, bias_send.at[i, 0], bias_recv.at[i], (t, shard)).wait_recv()
 
         bias_wide[...] = bias[...].astype(F32)
+        pltpu.make_async_copy(order_row, wanted, order_sem.at[0]).wait()
         for h in range(n - 1):
             pool_wait(h)
         early, late = (0, rows - block), (rows - block, rows)
@@ -448,6 +470,8 @@
         cross(1, *early)
         complete(comp_id)
         squeeze(*early)
+        for h in range(n - 1):
+            mix_copy(h).start()
         last(over_id)
         pool_wait(n - 1)
         gather(received_last, *late)
@@ -456,17 +480,18 @@
             cross(layer, *late)
         squeeze(*late)
         complete(over_id)
-        mix_local.wait()
         for k in range(1, n):
             source = lax.rem(z + k, n)
             view = joined.at[source]
             remote(view, view, mix_send.at[0], mix_recv.at[source], (t, shard)).wait_recv()
         wide = over_all.shape[4]
         for s in range(n_shard):
-            mixed = over_bias[:, s * wide:(s + 1) * wide].astype(F32)
-            for tower in range(n):
+            mixed = over_bias[s * wide:(s + 1) * wide].astype(F32).reshape(1, wide)
+            for k in range(n):
+                tower = lax.rem(z + k, n)
+                part_in = squeezed[n - 1] if k == 0 else joined[tower]
                 mixed = mixed + jnp.dot(
-                    joined[tower], over_all[tower, s // CORES, s % CORES], preferred_element_type=F32
+                    part_in, over_all[tower, s // CORES, s % CORES], preferred_element_type=F32
                 )
             out[:, s * wide:(s + 1) * wide] = jnp.maximum(mixed, 0.0).astype(BF16)
 
@@ -492,15 +517,14 @@
             for k in range(4):
                 second_copy(i, k).wait_send()
                 core_copy(i, k).wait_send()
-        for there in range(n):
-            @pl.when(z != there)
-            def _():
-                mix_copy(there).wait_send()
+        for h in range(n - 1):
+            mix_copy(h).wait_send()
 
         @pl.when(t == z)
         def _():
-            for k in range(1, n):
-                remote(bias_in, bias, bias_send.at[k], bias_recv.at[0], (turn(k), shard)).wait_send()
+            for i, (source, place) in enumerate(biases):
+                for k in range(1, n):
+                    remote(source, place, bias_send.at[i, k], bias_recv.at[i], (turn(k), shard)).wait_send()
 
     return kernel
 
@@ -511,23 +535,18 @@
 ):
     n = lax.axis_size("tower")
     n_shard = lax.axis_size("shard")
-    layer_id = lax.axis_index("shard") // CORES
     _, samples, slot_most, emb = pooled.shape
     layers, depth, rank = cross_down.shape[1:]
     width = cross_up.shape[3]
     cmp = comp_weight.shape[2]
     tables_each = width // emb
-    per_tower = tables_each * n_shard
     block = samples // (n_shard * n)
     rows = n * block
     out_width = over_bias.shape[0]
-    wanted = slot_order(table_tower, table_owner, layer_id, per_tower, slot_most)
     pool_view = jnp.transpose(pooled[0], (1, 0, 2)).reshape(slot_most, n, CORES, n, block, emb)
     down = cross_down[0].reshape(layers, n, depth // n, rank)
     up = cross_up[0].reshape(layers, n, rank // n, width)
     comp = comp_weight[0].reshape(n, depth // n, cmp)
-    bias_rows = jnp.concatenate([cross_bias[0].reshape(-1, emb), comp_bias[0].reshape(-1, emb)], axis=0)
-    bias_rows = jnp.pad(bias_rows, ((0, -bias_rows.shape[0] % 16), (0, 0)))
     weights = 2 * layers + 1
     dma = pltpu.SemaphoreType.DMA
     any_spec = pl.BlockSpec(memory_space=pl.ANY)
@@ -535,7 +554,7 @@
     result = pl.pallas_call(
         make_kernel(n, layers, tables_each, slot_most),
         out_shape=jax.ShapeDtypeStruct((block, out_width), BF16),
-        in_specs=[pl.BlockSpec(memory_space=pltpu.SMEM)] + [any_spec] * 6 + [vmem_spec],
+        in_specs=[vmem_spec] * 2 + [any_spec] * 7 + [vmem_spec],
         out_specs=vmem_spec,
         scratch_shapes=[
             pltpu.VMEM((layers, n, CORES, n, depth // n, rank), BF16),
@@ -553,8 +572,12 @@
             pltpu.VMEM((rows, rank), BF16),
             pltpu.VMEM((n, block, cmp), BF16),
             pltpu.VMEM((n, block, cmp), BF16),
-            pltpu.VMEM(bias_rows.shape, BF16),
-            pltpu.VMEM(bias_rows.shape, F32),
+            pltpu.VMEM(cross_bias.shape[1:], BF16),
+            pltpu.VMEM(comp_bias.shape, BF16),
+            pltpu.VMEM(cross_bias.shape[1:], F32),
+            pltpu.VMEM((1,) + table_tower.shape, jnp.int32),
+            pltpu.SMEM((1,) + table_tower.shape, jnp.int32),
+            dma((1,)),
             dma((weights, n)), dma((weights, n)),
             dma((weights, n)), dma((weights, n)),
             dma((weights + 1, n)), dma((weights + 1, n)),
@@ -563,13 +586,13 @@
             dma((n, n)), dma((n, n)),
             dma((n, n, CORES)), dma((n, n_shard)),
             dma((n,)), dma((n,)),
-            dma((n,)), dma((1,)),
+            dma((2, n)), dma((2,)),
         ],
         compiler_params=pltpu.CompilerParams(
             collective_id=0, has_side_effects=True, vmem_limit_bytes=60 * 1024 * 1024
         ),
         name="towers",
-    )(wanted, pool_view, down, up, comp, over_weight, bias_rows, over_bias.reshape(1, -1))
+    )(table_tower, table_owner, pool_view, down, up, comp, over_weight, cross_bias[0], comp_bias, over_bias)
     return result.reshape(1, block, out_width)
 
 

time: 203 us -> 187 us (0.921)
  the two profiles are of different devices: /device:TPU:30 before, /device:TPU:11 now
where the time goes in v3:
time: 187 us
  Pallas kernels  185 us (99%)
    pallas_call x1, Pallas kernels, turned(): pl.pallas_call(make_kernel(n, layers, tables_each, slot_most), out_shape=...  185 us

profile of v3, /device:TPU:11, one launch (start us, length us, event | category | flops | bytes accessed | tf_op | source)
XLA Modules:
  0.0 187.0 jit_solution(7216461398396128202)
XLA Ops:
  0.0 185.4 %towers.1 = bf16[96,1024]{1,0:T(8,128)(2,1)} custom-call(s32[128]{0:T(128)} %table_tower.1, s32[128]{0:T(128)} %table_owner.1, bf16[6,4,2,4,96,128]{5,4,3,2,1,0:T(8,128)(2,1)} %bitcast.10, bf16[2,4,128,512]{3,2,1,0:T(8,128)(2,1)} %bitcast.11, bf16[2,4,128,512]{3,2,1,0:T(8,128)(2,1)} %bitcast.12, bf16[4,128,256]{2,1,0:T(8,128)(2,1)} %bitcast.14, ...), custom_call_target="tpu_custom_call" | custom-call | tf_op jit(solution)/shard_map/towers/pallas_call | solution.py:554
  185.4 1.6 copy.12

commit v4 on v3

--- a/solution.py
+++ b/solution.py
@@ -400,47 +400,90 @@
                     (added[:, cols] + row).astype(BF16).reshape((hi - lo) // block, block, emb)
                 )
 
+        def sent():
+            for k in range(1, n):
+                over_copy(k).wait_send()
+                for h in range(n):
+                    pool_hop_copy(h, k).wait_send()
+                for i in range(weights):
+                    hop_copy(i, k).wait_send()
+            for k in range(n):
+                @pl.when(turn(k) != z)
+                def _():
+                    for i in range(weights):
+                        first_copy(i, k).wait_send()
+
+                pool_sent(k, range(n - 1))
+            for i in range(weights + 1):
+                for k in range(4):
+                    second_copy(i, k).wait_send()
+                    if i < weights:
+                        core_copy(i, k).wait_send()
+
+            @pl.when(t == z)
+            def _():
+                for i, (source, place) in enumerate(biases):
+                    for k in range(1, n):
+                        remote(source, place, bias_send.at[i, k], bias_recv.at[i], (turn(k), shard)).wait_send()
+
+        def pool_sent(k, chunks):
+            for core in range(CORES):
+                @pl.when(jnp.logical_or(turn(k) != z, c != core))
+                def _():
+                    for h in chunks:
+                        pool_copy(h, k, core).wait_send()
+
         comp_id, over_id = weights - 1, weights
+        early, late = (0, rows - block), (rows - block, rows)
+        first_start(1, 0)
         hop_start(comp_id)
-        for i in range(comp_id):
-            hop_start(i)
+        hop_start(0)
+        hop_on(comp_id)
+        hop_start(3)
+        first_start(0, 0)
+        first_start(comp_id, 0)
+        first_start(3, 0)
+        hop_on(0)
+        hop_start(1)
+        hop_start(2)
+        hop_on(1)
         pool_hop_start(0)
-        for i in (comp_id, 0, 1):
-            first_start(i, 0)
-        order_tables()
-        for i in (comp_id, 0, 1):
-            hop_on(i)
-        spread(comp_id)
+        hop_on(2)
         first_start(2, 0)
-        hop_on(2)
-        spread(0)
-        first_start(3, 0)
         hop_on(3)
+        pool_start(3, 0)
         over_local.start()
         for k in range(1, n):
             over_copy(k).start()
-        for h in range(n):
-            pool_start(h, 0)
+        spread(comp_id)
+        pool_hop_start(1)
+        spread(0)
+        pool_on(0)
+        pool_start(0, 0)
+        pool_start(2, 0)
+        pool_hop_start(2)
         spread(1)
-        pool_hop_start(1)
-        pool_on(0)
+        pool_start(1, 0)
         spread(2)
-        pool_hop_start(2)
+        relay(comp_id)
+        relay(0)
+        pool_on(1)
+        order_tables()
+        pool_hop_start(3)
         spread(3)
-        relay(comp_id)
-        pool_on(1)
-        relay(0)
         relay(1)
-        pool_hop_start(3)
         pool_on(2)
-        relay(2)
-        relay(3)
         over_wait()
         second_start(over_id)
+        relay(2)
+        last(comp_id)
+        relay(3)
+        pool_wait(0)
         pool_on(3)
-        last(comp_id)
+        last(1)
+        pool_wait(1)
         last(0)
-
+        pool_wait(2)
         for i, (source, place) in enumerate(biases):
             @pl.when(t == z)
             def _():
@@ -452,19 +495,15 @@
 
         bias_wide[...] = bias[...].astype(F32)
         pltpu.make_async_copy(order_row, wanted, order_sem.at[0]).wait()
-        for h in range(n - 1):
-            pool_wait(h)
-        early, late = (0, rows - block), (rows - block, rows)
         gather(received, *early)
         complete(0)
         lower(0, *early)
-        last(1)
         complete(1)
+        last(2)
         cross(0, *early)
-        last(2)
+        relay(over_id)
         complete(2)
         lower(1, *early)
-        relay(over_id)
         last(3)
         complete(3)
         cross(1, *early)
@@ -472,8 +511,9 @@
         squeeze(*early)
         for h in range(n - 1):
             mix_copy(h).start()
+        sent()
+        pool_wait(3)
         last(over_id)
-        pool_wait(n - 1)
         gather(received_last, *late)
         for layer in range(layers):
             lower(layer, *late)
@@ -495,36 +535,11 @@
                 )
             out[:, s * wide:(s + 1) * wide] = jnp.maximum(mixed, 0.0).astype(BF16)
 
-        for k in range(1, n):
-            over_copy(k).wait_send()
-            for h in range(n):
-                pool_hop_copy(h, k).wait_send()
-        for i in range(weights):
-            for k in range(1, n):
-                hop_copy(i, k).wait_send()
         for k in range(n):
-            @pl.when(turn(k) != z)
-            def _():
-                for i in range(weights):
-                    first_copy(i, k).wait_send()
-
-            for core in range(CORES):
-                @pl.when(jnp.logical_or(turn(k) != z, c != core))
-                def _():
-                    for h in range(n):
-                        pool_copy(h, k, core).wait_send()
-        for i in range(weights + 1):
-            for k in range(4):
-                second_copy(i, k).wait_send()
-                core_copy(i, k).wait_send()
+            pool_sent(k, (n - 1,))
+            core_copy(weights, k).wait_send()
         for h in range(n - 1):
             mix_copy(h).wait_send()
-
-        @pl.when(t == z)
-        def _():
-            for i, (source, place) in enumerate(biases):
-                for k in range(1, n):
-                    remote(source, place, bias_send.at[i, k], bias_recv.at[i], (turn(k), shard)).wait_send()
 
     return kernel
 

time: 187 us -> 181 us (0.968)
  the two profiles are of different devices: /device:TPU:11 before, /device:TPU:1 now
where the time goes in v4:
time: 181 us
  Pallas kernels  180 us (99%)
    pallas_call x1, Pallas kernels, turned(): pl.pallas_call(make_kernel(n, layers, tables_each, slot_most), out_shape=...  180 us

profile of v4, /device:TPU:1, one launch (start us, length us, event | category | flops | bytes accessed | tf_op | source)
XLA Modules:
  0.0 181.1 jit_solution(14525836263916389549)
XLA Ops:
  0.0 179.5 %towers.1 = bf16[96,1024]{1,0:T(8,128)(2,1)} custom-call(s32[128]{0:T(128)} %table_tower.1, s32[128]{0:T(128)} %table_owner.1, bf16[6,4,2,4,96,128]{5,4,3,2,1,0:T(8,128)(2,1)} %bitcast.10, bf16[2,4,128,512]{3,2,1,0:T(8,128)(2,1)} %bitcast.11, bf16[2,4,128,512]{3,2,1,0:T(8,128)(2,1)} %bitcast.12, bf16[4,128,256]{2,1,0:T(8,128)(2,1)} %bitcast.14, ...), custom_call_target="tpu_custom_call" | custom-call | tf_op jit(solution)/shard_map/towers/pallas_call | solution.py:569
  179.5 1.6 copy.12

commit v5 on v4

--- a/solution.py
+++ b/solution.py
@@ -369,8 +369,8 @@
         def cross(layer, lo, hi):
             current = base if layer == 0 else state
 
-            @pl.loop(0, blocks, unroll=True)
-            def _(s):
+            added = jnp.zeros((hi - lo, cmp), F32)
+            for s in range(blocks):
                 raised = jnp.dot(
                     lowered[lo:hi, :], up_all[layer, s // CORES, s % CORES].reshape(lowered.shape[1], width),
                     preferred_element_type=F32,
@@ -382,17 +382,18 @@
                         base[s, lo:hi, cols].astype(F32) * (raised[:, cols] + row)
                         + current[s, lo:hi, cols].astype(F32)
                     ).astype(BF16)
+                if layer == layers - 1:
+                    added = added + jnp.dot(
+                        state[s, lo:hi, :], comp_all[s // CORES, s % CORES].reshape(width, cmp),
+                        preferred_element_type=F32,
+                    )
+            return added
 
         def mix_copy(h):
             there = lax.rem(z + 1 + h, n)
             return remote(squeezed.at[h], joined.at[z], mix_send.at[h], mix_recv.at[z], (t, there * CORES + c))
 
-        def squeeze(lo, hi):
-            added = jnp.zeros((hi - lo, cmp), F32)
-            for s in range(blocks):
-                added = added + jnp.dot(
-                    state[s, lo:hi, :], comp_all[s // CORES, s % CORES].reshape(width, cmp), preferred_element_type=F32
-                )
+        def squeeze(lo, hi, added):
             for k in range(cmp // emb):
                 cols = slice(k * emb, (k + 1) * emb)
                 row = bias_low[:, cols].astype(F32)
@@ -506,9 +507,8 @@
         lower(1, *early)
         last(3)
         complete(3)
-        cross(1, *early)
         complete(comp_id)
-        squeeze(*early)
+        squeeze(*early, cross(1, *early))
         for h in range(n - 1):
             mix_copy(h).start()
         sent()
@@ -517,8 +517,8 @@
         gather(received_last, *late)
         for layer in range(layers):
             lower(layer, *late)
-            cross(layer, *late)
-        squeeze(*late)
+            added = cross(layer, *late)
+        squeeze(*late, added)
         complete(over_id)
         for k in range(1, n):
             source = lax.rem(z + k, n)

time: 181 us -> 181 us (level)
  no operation moved by 1% of the time
where the time goes in v5:
time: 181 us; the launch traced here: 180 us
  Pallas kernels  179 us (99%)
    pallas_call x1, Pallas kernels, turned(): pl.pallas_call(make_kernel(n, layers, tables_each, slot_most), out_shape=...  179 us

profile of v5, /device:TPU:1, one launch (start us, length us, event | category | flops | bytes accessed | tf_op | source)
XLA Modules:
  0.0 180.5 jit_solution(18231376469943952005)
XLA Ops:
  0.0 178.8 %towers.1 = bf16[96,1024]{1,0:T(8,128)(2,1)} custom-call(s32[128]{0:T(128)} %table_tower.1, s32[128]{0:T(128)} %table_owner.1, bf16[6,4,2,4,96,128]{5,4,3,2,1,0:T(8,128)(2,1)} %bitcast.10, bf16[2,4,128,512]{3,2,1,0:T(8,128)(2,1)} %bitcast.11, bf16[2,4,128,512]{3,2,1,0:T(8,128)(2,1)} %bitcast.12, bf16[4,128,256]{2,1,0:T(8,128)(2,1)} %bitcast.14, ...), custom_call_target="tpu_custom_call" | custom-call | tf_op jit(solution)/shard_map/towers/pallas_call | solution.py:569
  178.8 1.6 copy.12

commit v6 on v5

--- a/solution.py
+++ b/solution.py
@@ -520,18 +520,22 @@
             added = cross(layer, *late)
         squeeze(*late, added)
         complete(over_id)
+        wide = over_all.shape[4]
+        begun = [
+            over_bias[s * wide:(s + 1) * wide].astype(F32).reshape(1, wide)
+            + jnp.dot(squeezed[n - 1], over_all[z, s // CORES, s % CORES], preferred_element_type=F32)
+            for s in range(n_shard)
+        ]
         for k in range(1, n):
             source = lax.rem(z + k, n)
             view = joined.at[source]
             remote(view, view, mix_send.at[0], mix_recv.at[source], (t, shard)).wait_recv()
-        wide = over_all.shape[4]
         for s in range(n_shard):
-            mixed = over_bias[s * wide:(s + 1) * wide].astype(F32).reshape(1, wide)
-            for k in range(n):
+            mixed = begun[s]
+            for k in range(1, n):
                 tower = lax.rem(z + k, n)
-                part_in = squeezed[n - 1] if k == 0 else joined[tower]
                 mixed = mixed + jnp.dot(
-                    part_in, over_all[tower, s // CORES, s % CORES], preferred_element_type=F32
+                    joined[tower], over_all[tower, s // CORES, s % CORES], preferred_element_type=F32
                 )
             out[:, s * wide:(s + 1) * wide] = jnp.maximum(mixed, 0.0).astype(BF16)
 

time: 181 us -> 181 us (level)
  no operation moved by 1% of the time
where the time goes in v6:
time: 181 us
  Pallas kernels  179 us (99%)
    pallas_call x1, Pallas kernels, turned(): pl.pallas_call(make_kernel(n, layers, tables_each, slot_most), out_shape=...  179 us

profile of v6, /device:TPU:1, one launch (start us, length us, event | category | flops | bytes accessed | tf_op | source)
XLA Modules:
  0.0 180.6 jit_solution(17533900672117121341)
XLA Ops:
  0.0 179.0 %towers.1 = bf16[96,1024]{1,0:T(8,128)(2,1)} custom-call(s32[128]{0:T(128)} %table_tower.1, s32[128]{0:T(128)} %table_owner.1, bf16[6,4,2,4,96,128]{5,4,3,2,1,0:T(8,128)(2,1)} %bitcast.10, bf16[2,4,128,512]{3,2,1,0:T(8,128)(2,1)} %bitcast.11, bf16[2,4,128,512]{3,2,1,0:T(8,128)(2,1)} %bitcast.12, bf16[4,128,256]{2,1,0:T(8,128)(2,1)} %bitcast.14, ...), custom_call_target="tpu_custom_call" | custom-call | tf_op jit(solution)/shard_map/towers/pallas_call | solution.py:573
  179.0 1.6 copy.12
